TPU v7x, 32 devices: a whole 2x2x4 slice. The times are simulated.
32 devices in a mesh: group: 1, req: 4 (over z), head: 4 (over y, x), pool: 2 (over core).
Axes of the slice: x: 2, y: 2, z: 4, core: 2. Of those that a mesh axis runs over, the one named last changes fastest.
Arguments:
- queries: bfloat16 [192, 4096], P(('group', 'req'), 'head'), may hold values from -128 to 128
- new_entries: bfloat16 [192, 2, 4, 256], P(('group', 'req'), None, 'head'), may hold values from -6 to 6
- cache_pages: bfloat16 [4, 416, 16, 256], P('head', ('group', 'req', 'pool')), may hold values from -6 to 6
- page_table: int32 [192, 2, 1], P(('group', 'req'), 'pool'), may hold values from 0 to 51, as said below
- cached_length: int32 [192, 2], P(('group', 'req'), 'pool'), may hold values from 1 to 16, as said below
- leave_slots: int32 [32], P(('group', 'req', 'pool')), may hold values from 0 to 50, as said below
- arrive_slots: int32 [32], P(('group', 'req', 'pool')), may hold values from 0 to 51, as said below
- residual: bfloat16 [192, 2048], P(('group', 'req', 'head')), may hold values from -5 to 5
- norm_gain: float32 [2048], replicated, may hold values from 0.5 to 1.5
- output_weight: bfloat16 [4096, 2048], P(('head', 'pool')), may hold values from -0.25 to 0.25
- expert_choice: int32 [192, 8], P(('group', 'req', 'head')), may hold values from 0 to 15, all different within a row; in each aligned block of 12 rows (0 to 11, 12 to 23, ...) at most 12 rows name the same one
- route_weight: float32 [192, 8], P(('group', 'req', 'head')), may hold values from 0.2 to 1
- gate_up: bfloat16 [16, 2, 384, 2048], P(('req', 'head'), None, 'pool'), may hold values from -0.125 to 0.125
- down_weight: bfloat16 [16, 384, 2048], P(('req', 'head'), 'pool'), may hold values from -0.3125 to 0.3125
Outputs:
- decoded: bfloat16 [192, 2048], P(('group', 'req', 'head'), 'pool')
Inputs may be any that keep to these rules, and one draw needn't show every extreme that they name: `page_table`: within each block of one index of req and one pool, the 48 entries name distinct slots, none of them among that block's leave_slots. `leave_slots`: each block's 4 entries are distinct. `arrive_slots`: each block's 4 entries are distinct slots that its page table names. `cached_length`: in every block of 48 requests and each pool some request has 16. `expert_choice`: each row names 8 distinct experts; in each aligned block of 12 rows no expert is named more than 12 times, a bound that some block reaches.
All inputs are finite; a program needn't handle non-finite values.
Results may differ from a plain program's by a relative error of at most 0.023.
Values may be sent and summed in bfloat16 or wider, within the bound.
A program may use at most 64 MiB of HBM per device.

v0:
```python
import jax
import jax.numpy as jnp
from jax import lax
from jax.sharding import PartitionSpec as P


def swapped(value, axis, apart):
    mask = 2**apart
    pairs = [(source, source ^ mask) for source in range(lax.axis_size(axis))]
    return lax.ppermute(value, axis, pairs)


def combined_all(shard, axis, join):
    gathered = jax.tree.map(
        lambda a, kind: lax.all_gather(a.astype(kind), axis),
        shard,
        (jnp.bfloat16, jnp.bfloat16, jnp.bfloat16),
    )

    def take(source):
        return jax.tree.map(
            lambda a, own: lax.dynamic_index_in_dim(a, source, 0, False).astype(own.dtype),
            gathered,
            shard,
        )

    return lax.fori_loop(
        1, lax.axis_size(axis), lambda source, state: join(state, take(source)), take(0)
    )


def merge_parts(earlier, later):
    first_max, first_denominator, first_value = earlier
    second_max, second_denominator, second_value = later
    largest = jnp.maximum(first_max, second_max)
    first_scale = jnp.exp(first_max - largest)
    second_scale = jnp.exp(second_max - largest)
    denominator = first_denominator * first_scale + second_denominator * second_scale
    weighted = first_value * first_scale[..., None] + second_value * second_scale[..., None]
    return (largest, denominator, weighted)


def local(
    queries,
    new_entries,
    cache_pages,
    page_table,
    cached_length,
    leave_slots,
    arrive_slots,
    residual,
    norm_gain,
    output_weight,
    expert_choice,
    route_weight,
    gate_up,
    down_weight,
):
    batch_size = queries.shape[0]
    group_count = cache_pages.shape[0]
    head_dim = new_entries.shape[3] // 2
    group_size = queries.shape[1] // (group_count * head_dim)
    pool_index = lax.axis_index("pool")
    outgoing = cache_pages[:, leave_slots]
    arrived = swapped(outgoing, "pool", 0)
    current = cache_pages.at[:, arrive_slots].set(arrived)
    context = current[:, page_table[:, 0, :]]
    context = context.reshape(group_count, batch_size, -1, 2 * head_dim)
    context_keys = context[..., :head_dim]
    context_values = context[..., head_dim:]
    grouped_queries = queries.reshape(batch_size, group_count, group_size, head_dim)
    score_scale = head_dim ** (-0.5)
    attention_scores = (
        jnp.einsum(
            "bgqd,gbtd->bgqt", grouped_queries, context_keys, preferred_element_type=jnp.float32
        )
        * score_scale
    )
    positions = jnp.arange(context.shape[2], dtype=jnp.int32)
    valid_mask = positions[None, :] < cached_length
    attention_scores = jnp.where(valid_mask[:, None, None, :], attention_scores, -jnp.inf)
    fresh_scores = (
        jnp.einsum(
            "bgqd,bsgd->bgqs",
            grouped_queries,
            new_entries[..., :head_dim],
            preferred_element_type=jnp.float32,
        )
        * score_scale
    )
    fresh_scores = jnp.where(pool_index == 0, fresh_scores, -jnp.inf)
    largest = jnp.maximum(jnp.max(attention_scores, axis=-1), jnp.max(fresh_scores, axis=-1))
    local_weights = jnp.exp(attention_scores - largest[..., None])
    fresh_weights = jnp.exp(fresh_scores - largest[..., None])
    denominator = jnp.sum(local_weights, axis=-1) + jnp.sum(fresh_weights, axis=-1)
    weighted = jnp.einsum("bgqt,gbtd->bgqd", local_weights, context_values.astype(jnp.float32))
    weighted = weighted + jnp.einsum(
        "bgqs,bsgd->bgqd", fresh_weights, new_entries[..., head_dim:].astype(jnp.float32)
    )
    largest, denominator, weighted = combined_all(
        (largest, denominator, weighted), "pool", merge_parts
    )
    attended = (weighted / denominator[..., None]).reshape(batch_size, -1).astype(jnp.bfloat16)
    head_width = output_weight.shape[0]
    own_heads = lax.dynamic_slice_in_dim(attended, pool_index * head_width, head_width, 1)
    partial_value = jnp.dot(own_heads, output_weight, preferred_element_type=jnp.float32)
    rows_here = residual.shape[0]
    summed = lax.psum(partial_value.astype(jnp.bfloat16), ("head", "pool")).astype(jnp.float32)
    attention = lax.dynamic_slice_in_dim(summed, lax.axis_index("head") * rows_here, rows_here, 0)
    hidden = residual.astype(jnp.float32) + attention
    normed = (
        hidden * lax.rsqrt(jnp.mean(hidden * hidden, axis=-1, keepdims=True) + 1e-06) * norm_gain
    ).astype(jnp.bfloat16)
    expert_count = lax.axis_size("req") * lax.axis_size("head")
    top_count = expert_choice.shape[1]
    capacity = max(
        2, min(rows_here, (2 * rows_here * top_count + expert_count - 1) // expert_count)
    )
    flat_choice = expert_choice.reshape(-1)
    expert_hits = (
        flat_choice[:, None] == jnp.arange(expert_count, dtype=jnp.int32)[None, :]
    ).astype(jnp.int32)
    earlier = jnp.cumsum(expert_hits, axis=0) - expert_hits
    slot_index = jnp.sum(earlier * expert_hits, axis=1)
    target = flat_choice * capacity + slot_index
    placed = (
        target[:, None] == jnp.arange(expert_count * capacity, dtype=jnp.int32)[None, :]
    ).astype(jnp.float32)
    placed = placed.reshape(rows_here, top_count, expert_count * capacity)
    dispatch = jnp.sum(placed, axis=1).astype(jnp.bfloat16)
    combine_matrix = jnp.sum(placed * route_weight[:, :, None], axis=1)
    outgoing_rows = jnp.einsum("re,rd->ed", dispatch, normed, preferred_element_type=jnp.float32)
    outgoing_rows = outgoing_rows.astype(jnp.bfloat16).reshape(expert_count, capacity, -1)
    model_width = normed.shape[1]
    half_width = model_width // lax.axis_size("pool")
    projection = gate_up[0].reshape(-1, model_width)
    hidden_size = projection.shape[0] // 2
    received = lax.all_to_all(
        outgoing_rows, ("req", "head"), split_axis=0, concat_axis=0, tiled=True
    )
    sources = received.shape[0]
    item_count = received.shape[1]
    flat_rows = received.reshape(sources * item_count, model_width)
    projected = jnp.einsum("nd,fd->nf", flat_rows, projection, preferred_element_type=jnp.float32)
    activated = (jax.nn.silu(projected[:, :hidden_size]) * projected[:, hidden_size:]).astype(
        jnp.bfloat16
    )
    part_sum = jnp.dot(activated, down_weight[0], preferred_element_type=jnp.float32).reshape(
        sources, item_count, model_width
    )
    column_sum = lax.psum_scatter(
        part_sum.astype(jnp.bfloat16), "pool", scatter_dimension=2, tiled=True
    )
    returned = lax.all_to_all(column_sum, ("req", "head"), split_axis=0, concat_axis=0, tiled=True)
    gathered = returned.reshape(expert_count * capacity, half_width).astype(jnp.float32)
    expert_mix = jnp.dot(combine_matrix, gathered, precision=lax.Precision.HIGHEST)
    own_columns = lax.dynamic_slice_in_dim(hidden, pool_index * half_width, half_width, 1)
    return (own_columns + expert_mix).astype(jnp.bfloat16)


def solution(mesh):
    return jax.shard_map(
        local,
        mesh=mesh,
        in_specs=(
            P(("group", "req"), "head"),
            P(("group", "req"), None, "head", None),
            P("head", ("group", "req", "pool"), None, None),
            P(("group", "req"), "pool", None),
            P(("group", "req"), "pool"),
            P(("group", "req", "pool")),
            P(("group", "req", "pool")),
            P(("group", "req", "head"), None),
            P(),
            P(("head", "pool"), None),
            P(("group", "req", "head"), None),
            P(("group", "req", "head"), None),
            P(("req", "head"), None, "pool", None),
            P(("req", "head"), "pool", None),
        ),
        out_specs=P(("group", "req", "head"), "pool"),
        check_vma=False,
    )
```

profile of v0, /device:TPU:0, one launch (start us, length us, event | category | flops | bytes accessed | tf_op | source)
XLA Modules:
  0.0 159.7 jit_solution(2999815218880634779)
XLA Ops:
  6.5 0.0 copy-start
  6.5 0.0 copy-start.2
  6.5 0.0 copy-start.4
  6.5 0.0 all-reduce.2.cloned.1.call-start
  6.5 1.2 copy.73
  7.7 0.7 compare_select_fusion.1
  8.4 0.5 gather_fusion
  8.9 0.6 collective-permute-start
  9.5 0.7 fusion.23
  10.2 0.7 compare_select_fusion.2
  10.8 0.7 iota_compare_fusion.2
  11.5 0.8 copy.59
  12.3 0.1 eq.33
  12.4 0.1 fusion.12
  12.5 0.1 reduce_window_sum.11
  12.6 0.2 select_reduce_fusion.1
  12.8 0.1 reduce_sum.59
  12.9 0.9 copy.64
  13.8 1.0 fusion.25
  14.8 0.0 copy-done.4
  14.8 0.1 copy.61
  14.9 0.0 collective-permute-done
  14.9 0.6 scatter_fusion
  15.5 0.6 gather_fusion.1
  16.1 0.3 fusion.24
  16.4 0.1 fusion.14
  16.5 0.0 copy-done.2
  16.6 0.2 fusion.15
  16.8 0.1 copy.54
  16.9 1.8 %all-gather.3 = bf16[2,48,8]{1,2,0:T(8,128)(2,1)S(1)} all-gather(bf16[1,48,8]{1,2,0:T(8,128)(2,1)S(1)} %copy.54), channel_id=3, replica_groups=mesh['group'=1,'req'=4,'head'=4,'pool'=2] {'pool'}, dimensions={0}, use_global_device_ids=true | all-gather | bytes 2304 | tf_op jit(solution)/shard_map/all_gather | solution.py:15
  18.7 0.2 fusion.7
  18.9 0.1 copy.57
  19.0 1.8 %all-gather.4 = bf16[2,48,8]{1,2,0:T(8,128)(2,1)S(1)} all-gather(bf16[1,48,8]{1,2,0:T(8,128)(2,1)S(1)} %copy.57), channel_id=4, replica_groups=mesh['group'=1,'req'=4,'head'=4,'pool'=2] {'pool'}, dimensions={0}, use_global_device_ids=true | all-gather | bytes 2304 | tf_op jit(solution)/shard_map/all_gather | solution.py:15
  20.9 0.1 copy.55
  21.0 0.1 copy.58
  21.0 0.1 copy.56
  21.1 0.3 fusion.2
  21.4 1.9 %all-gather = bf16[96,8,128]{2,1,0:T(8,128)(2,1)S(1)} all-gather(bf16[48,8,128]{2,1,0:T(8,128)(2,1)S(1)} %fusion.2), channel_id=2, replica_groups=mesh['group'=1,'req'=4,'head'=4,'pool'=2] {'pool'}, dimensions={0}, use_global_device_ids=true | all-gather | bytes 294912 | tf_op jit(solution)/shard_map/all_gather | solution.py:15
  23.3 0.0 copy-start.1
  23.3 0.2 divide_convert_fusion
  23.6 0.0 copy-start.3
  23.6 0.0 copy-done
  23.6 1.2 convolution_convert_fusion.2
  24.8 0.0 all-reduce.2.cloned.1.call-update
  24.8 0.0 reduce-scatter.2.cloned.1.call-start
  24.8 0.1 convert_reduce_fusion
  25.0 56.1 %all-reduce.2.cloned.1.call-done = bf16[48,2048]{1,0:T(8,128)(2,1)} async-done(((bf16[48,2048]{1,0:T(8,128)(2,1)}), bf16[48,2048]{1,0:T(8,128)(2,1)}) %all-reduce.2.cloned.1.call-update) | async-done | bytes 196624 | tf_op jit(solution)/shard_map/psum | solution.py:108
  81.0 0.0 copy-done.1
  81.0 1.0 multiply_reduce_fusion
  82.1 0.0 copy-done.3
  82.1 1.3 convolution_convert_fusion.1
  83.4 1.3 reshape.273
  84.6 30.5 %all_to_all.10 = bf16[16,12,2048]{2,1,0:T(8,128)(2,1)} all-to-all(bf16[16,12,2048]{2,1,0:T(8,128)(2,1)S(1)} %reshape.273), channel_id=1, replica_groups=mesh['group'=1,'req'=4,'head'=4,'pool'=2] {'req','head'}, dimensions={0} | all-to-all | bytes 1572864 | tf_op jit(solution)/shard_map/all_to_all | solution.py:138
  115.1 1.3 reshape.274
  116.4 2.1 %fusion.26 = f32[192,384]{1,0:T(8,128)S(1)} fusion(bf16[192,2048]{1,0:T(8,128)(2,1)S(1)} %reshape.274, bf16[384,2048]{1,0:T(8,128)(2,1)} %bitcast.85), kind=kOutput, calls=%fused_computation.71 | convolution fusion | flops 301989888 | bytes 2654208 | tf_op jit(solution)/shard_map/nd,fd->nf/dot_general | solution.py:144
  118.5 0.1 fusion.6
  118.7 2.4 %convolution_convert_fusion = bf16[16,12,2048]{2,0,1:T(8,128)(2,1)} fusion(bf16[1,192,2048]{2,1,0:T(8,128)(2,1)} %param.27, bf16[16,12,192]{2,1,0:T(8,128)(2,1)S(1)} %dot_general.36), kind=kOutput, calls=%fused_computation.3 | convolution fusion | flops 151388160 | bytes 1646592 | tf_op jit(solution)/shard_map/dot_general | solution.py:148
  121.0 0.0 reduce-scatter.2.cloned.1.call-update
  121.1 6.6 %reduce-scatter.2.cloned.1.call-done = bf16[16,12,1024]{2,0,1:T(8,128)(2,1)} async-done(((bf16[16,12,2048]{2,0,1:T(8,128)(2,1)}), bf16[16,12,1024]{2,0,1:T(8,128)(2,1)}) %reduce-scatter.2.cloned.1.call-update) | async-done | bytes 393232 | tf_op jit(solution)/shard_map/reduce_scatter | solution.py:151
  127.6 2.0 %copy.63 = bf16[16,12,1024]{2,1,0:T(8,128)(2,1)} copy(bf16[16,12,1024]{2,0,1:T(8,128)(2,1)} %reduce-scatter.2.cloned.1.call-done) | data formatting | bytes 786432 | tf_op jit(solution)/shard_map/reduce_scatter | solution.py:151
  129.6 6.7 %all-to-all-start.1 = ((bf16[16,12,1024]{2,1,0:T(8,128)(2,1)}), bf16[16,12,1024]{2,1,0:T(8,128)(2,1)S(1)}, u32[]{:S(2)}, u32[]{:S(2)}) async-start(bf16[16,12,1024]{2,1,0:T(8,128)(2,1)} %copy.63), calls=%async_computation.2 | async-start | bytes 1048576 | tf_op jit(solution)/shard_map/all_to_all | solution.py:154
  136.4 15.5 %all-to-all-done.1 = bf16[16,12,1024]{2,1,0:T(8,128)(2,1)S(1)} async-done(((bf16[16,12,1024]{2,1,0:T(8,128)(2,1)}), bf16[16,12,1024]{2,1,0:T(8,128)(2,1)S(1)}, u32[]{:S(2)}, u32[]{:S(2)}) %all-to-all-start.1) | async-done | bytes 393248 | tf_op jit(solution)/shard_map/all_to_all | solution.py:154
  151.9 0.1 reshape.275
  151.9 0.9 fusion.4
  (9 shorter events, 0.1 us)
Async XLA Ops:
  6.5 17.1 %copy-start = (bf16[512,2048]{1,0:T(8,128)(2,1)S(1)}, bf16[512,2048]{1,0:T(8,128)(2,1)}, u32[]{:S(2)}) copy-start(bf16[512,2048]{1,0:T(8,128)(2,1)} %param.23) | copy-start | bytes 6291460
  6.5 10.0 %copy-start.2 = (bf16[48,2,1,256]{3,1,2,0:T(2,128)(2,1)S(1)}, bf16[48,2,1,256]{3,1,2,0:T(2,128)(2,1)}, u32[]{:S(2)}) copy-start(bf16[48,2,1,256]{3,1,2,0:T(2,128)(2,1)} %param.15) | copy-start | bytes 147460
  6.5 8.3 %copy-start.4 = (f32[12,8]{0,1:T(8,128)S(1)}, f32[12,8]{0,1:T(8,128)}, u32[]{:S(2)}) copy-start(f32[12,8]{0,1:T(8,128)} %param.25) | copy-start | bytes 1156
  6.5 74.5 %all-reduce.2.cloned.1.call-start = ((), (), s32[]{:S(2)}) async-start(), calls=%async_computation.3 | async-start | bytes 393216 | tf_op jit(solution)/shard_map/psum | solution.py:108
  8.9 6.0 %collective-permute-start = (bf16[1,4,16,256]{3,2,1,0:T(8,128)(2,1)S(1)}, bf16[1,4,16,256]{3,2,1,0:T(8,128)(2,1)S(1)}, u32[]{:S(2)}, u32[]{:S(2)}) collective-permute-start(bf16[1,4,16,256]{3,2,1,0:T(8,128)(2,1)S(1)} %bitcast.94), channel_id=1, source_target_pairs={{0,1},{1,0},{2,3},{3,2},{4,5},{5,4},{6,7},{7,6},{8,9},{9,8},{10,11... | collective-permute-start | bytes 98312 | tf_op jit(solution)/shard_map/ppermute | solution.py:10
  23.3 57.7 %copy-start.1 = (bf16[12,2048]{1,0:T(8,128)(2,1)S(1)}, bf16[12,2048]{1,0:T(8,128)(2,1)}, u32[]{:S(2)}) copy-start(bf16[12,2048]{1,0:T(8,128)(2,1)} %param.21) | copy-start | bytes 147460
  23.6 58.5 %copy-start.3 = (f32[2048]{0:T(1024)S(1)}, f32[2048]{0:T(1024)}, u32[]{:S(2)}) copy-start(f32[2048]{0:T(1024)} %param.22) | copy-start | bytes 24580
  24.8 102.8 %reduce-scatter.2.cloned.1.call-start = ((), (), s32[]{:S(2)}) async-start(), calls=%async_computation.4 | async-start | bytes 1179648 | tf_op jit(solution)/shard_map/reduce_scatter | solution.py:151
  129.6 22.2 %all-to-all-start.1 = ((bf16[16,12,1024]{2,1,0:T(8,128)(2,1)}), bf16[16,12,1024]{2,1,0:T(8,128)(2,1)S(1)}, u32[]{:S(2)}, u32[]{:S(2)}) async-start(bf16[16,12,1024]{2,1,0:T(8,128)(2,1)} %copy.63), calls=%async_computation.2 | async-start | bytes 1048576 | tf_op jit(solution)/shard_map/all_to_all | solution.py:154
Sparse Core Ops, SparseCore 0:
  24.9 56.0 all-reduce.1
  121.2 6.3 reduce-scatter.1
where the time goes:
time: 160 us
  waiting for transfers between devices  78.1 us (49%)
  blocking collectives  36.1 us (23%)
  between operations  13.6 us (8%)
  local copies, waits for them, and re-layouts  10 us (6%)
  matrix products  9.56 us (6%)
  starting transfers between devices  7.33 us (5%)
  other arithmetic  4.95 us (3%)
    psum x1, waiting for transfers between devices, local(): lax.psum(partial_value.astype(jnp.bfloat16), ('head', 'pool'))  56.1 us
    all_to_all x1, blocking collectives, local(): lax.all_to_all(outgoing_rows, ('req', 'head'), split_axis=0, concat_axis=...  30.5 us
    all_to_all x1, waiting for transfers between devices, local(): lax.all_to_all(column_sum, ('req', 'head'), split_axis=0, concat_axis=0,...  15.5 us
    all_to_all x1, starting transfers between devices, local(): lax.all_to_all(column_sum, ('req', 'head'), split_axis=0, concat_axis=0,...  6.73 us
    reduce_scatter x1, waiting for transfers between devices, local(): lax.psum_scatter(part_sum.astype(jnp.bfloat16), 'pool', scatter_dimension...  6.55 us
    all_gather x3, blocking collectives, combined_all(): lax.all_gather(a.astype(kind), axis)  5.63 us
  transfers between devices with their start and end apart: 4, of which 3 were waited for; matrix products, arithmetic and copies ran while one was open for 3% of the time, Pallas kernels for 0%

commit v1 on v0

--- a/solution.py
+++ b/solution.py
@@ -105,7 +105,11 @@
     own_heads = lax.dynamic_slice_in_dim(attended, pool_index * head_width, head_width, 1)
     partial_value = jnp.dot(own_heads, output_weight, preferred_element_type=jnp.float32)
     rows_here = residual.shape[0]
-    summed = lax.psum(partial_value.astype(jnp.bfloat16), ("head", "pool")).astype(jnp.float32)
+    summed = (
+        lax.all_gather(partial_value.astype(jnp.bfloat16), axis_name=("head", "pool"))
+        .sum(axis=0)
+        .astype(jnp.float32)
+    )
     attention = lax.dynamic_slice_in_dim(summed, lax.axis_index("head") * rows_here, rows_here, 0)
     hidden = residual.astype(jnp.float32) + attention
     normed = (

time: 160 us -> 133 us (0.83)
  waiting for transfers between devices: 78.1 us -> 49.3 us
  blocking collectives: 36.1 us -> 37.9 us
    psum x1 -> x0, waiting for transfers between devices: 56.1 us -> none  [local(): lax.psum(partial_value.astype(jnp.bfloat16), ('head', 'pool'))]
    all_gather x0 -> x1, waiting for transfers between devices: none -> 27.1 us  [local(): lax.all_gather(partial_value.astype(jnp.bfloat16), axis_name=('head', 'po...]
    all_to_all x1, blocking collectives: 30.5 us -> 32.2 us  [local(): lax.all_to_all(outgoing_rows, ('req', 'head'), split_axis=0, concat_axis=...]
    reduce_sum x0 -> x1, other arithmetic: none -> 1.65 us  [local(): summed = lax.all_gather(partial_value.astype(jnp.bfloat16), axis_name=('h...]
  transfers between devices with their start and end apart: 4 -> 4, of which waited for: 3 -> 3; matrix products, arithmetic and copies ran while one was open for 3% -> 4% of each run, Pallas kernels for 0% -> 0%
where the time goes in v1:
time: 133 us
  waiting for transfers between devices  49.3 us (37%)
  blocking collectives  37.9 us (28%)
  between operations  13.7 us (10%)
  matrix products  9.56 us (7%)
  local copies, waits for them, and re-layouts  9.3 us (7%)
  starting transfers between devices  7.34 us (6%)
  other arithmetic  5.73 us (4%)
    all_to_all x1, blocking collectives, local(): lax.all_to_all(outgoing_rows, ('req', 'head'), split_axis=0, concat_axis=...  32.2 us
    all_gather x1, waiting for transfers between devices, local(): lax.all_gather(partial_value.astype(jnp.bfloat16), axis_name=('head', 'po...  27.1 us
    all_to_all x1, waiting for transfers between devices, local(): lax.all_to_all(column_sum, ('req', 'head'), split_axis=0, concat_axis=0,...  15.5 us
    all_to_all x1, starting transfers between devices, local(): lax.all_to_all(column_sum, ('req', 'head'), split_axis=0, concat_axis=0,...  6.74 us
    reduce_scatter x1, waiting for transfers between devices, local(): lax.psum_scatter(part_sum.astype(jnp.bfloat16), 'pool', scatter_dimension...  6.64 us
    all_gather x3, blocking collectives, combined_all(): lax.all_gather(a.astype(kind), axis)  5.63 us
  transfers between devices with their start and end apart: 4, of which 3 were waited for; matrix products, arithmetic and copies ran while one was open for 4% of the time, Pallas kernels for 0%

profile of v1, /device:TPU:0, one launch (start us, length us, event | category | flops | bytes accessed | tf_op | source)
XLA Modules:
  0.0 132.8 jit_solution(10844197944778628042)
XLA Ops:
  6.5 0.0 copy-start
  6.5 0.0 copy-start.2
  6.5 0.0 all-gather.8.cloned.1.call-start
  6.5 1.2 copy.72
  7.7 0.7 compare_select_fusion.1
  8.4 0.5 gather_fusion
  8.9 0.6 collective-permute-start
  9.5 0.7 fusion.23
  10.2 0.7 compare_select_fusion.2
  10.8 0.7 iota_compare_fusion.2
  11.5 0.9 copy.64
  12.5 1.0 fusion.25
  13.4 0.0 collective-permute-done
  13.4 0.6 scatter_fusion
  14.1 0.6 gather_fusion.1
  14.7 0.3 fusion.24
  15.0 0.1 fusion.14
  15.1 0.0 copy-done.2
  15.1 0.2 fusion.15
  15.3 0.1 copy.54
  15.4 1.8 %all-gather.4 = bf16[2,48,8]{1,2,0:T(8,128)(2,1)S(1)} all-gather(bf16[1,48,8]{1,2,0:T(8,128)(2,1)S(1)} %copy.54), channel_id=3, replica_groups=mesh['group'=1,'req'=4,'head'=4,'pool'=2] {'pool'}, dimensions={0}, use_global_device_ids=true | all-gather | bytes 2304 | tf_op jit(solution)/shard_map/all_gather | solution.py:15
  17.3 0.2 fusion.7
  17.5 0.1 copy.57
  17.6 1.8 %all-gather.5 = bf16[2,48,8]{1,2,0:T(8,128)(2,1)S(1)} all-gather(bf16[1,48,8]{1,2,0:T(8,128)(2,1)S(1)} %copy.57), channel_id=4, replica_groups=mesh['group'=1,'req'=4,'head'=4,'pool'=2] {'pool'}, dimensions={0}, use_global_device_ids=true | all-gather | bytes 2304 | tf_op jit(solution)/shard_map/all_gather | solution.py:15
  19.4 0.1 copy.55
  19.5 0.1 copy.58
  19.6 0.1 copy.56
  19.6 0.3 fusion.2
  19.9 1.9 %all-gather = bf16[96,8,128]{2,1,0:T(8,128)(2,1)S(1)} all-gather(bf16[48,8,128]{2,1,0:T(8,128)(2,1)S(1)} %fusion.2), channel_id=2, replica_groups=mesh['group'=1,'req'=4,'head'=4,'pool'=2] {'pool'}, dimensions={0}, use_global_device_ids=true | all-gather | bytes 294912 | tf_op jit(solution)/shard_map/all_gather | solution.py:15
  21.9 0.0 copy-start.4
  21.9 0.2 divide_convert_fusion
  22.1 0.0 copy-done
  22.1 1.2 convolution_convert_fusion.2
  23.3 0.0 all-gather.8.cloned.1.call-update
  23.3 0.0 reduce-scatter.2.cloned.1.call-start
  23.4 0.0 copy-done.4
  23.4 0.1 copy.59
  23.5 0.1 eq.33
  23.5 0.0 copy-done.5
  23.6 0.1 copy.61
  23.6 0.1 fusion.12
  23.7 0.1 reduce_window_sum.11
  23.9 0.2 select_reduce_fusion.1
  24.0 0.1 reduce_sum.72
  24.1 0.1 convert_reduce_fusion
  24.3 27.1 %all-gather.8.cloned.1.call-done = bf16[384,2048]{1,0:T(8,128)(2,1)} async-done(((bf16[48,2048]{1,0:T(8,128)(2,1)}), bf16[384,2048]{1,0:T(8,128)(2,1)}) %all-gather.8.cloned.1.call-update) | async-done | bytes 1572880 | tf_op jit(solution)/shard_map/all_gather | solution.py:109
  51.4 1.7 %reduce_sum.70 = bf16[48,2048]{1,0:T(8,128)(2,1)S(1)} reduce(bf16[8,48,2048]{2,1,0:T(8,128)(2,1)} %bitcast.86, bf16[]{:T(256)} %constant.64.clone.1), dimensions={0}, to_apply=%region_5.6 | reduce | flops 688128 | bytes 1769474 | tf_op jit(solution)/shard_map/reduce_sum | solution.py:110
  53.1 0.0 copy-done.1
  53.1 0.2 multiply_reduce_fusion
  53.3 0.0 copy-done.3
  53.3 1.3 convolution_convert_fusion.1
  54.6 1.3 reshape.273
  55.8 32.2 %all_to_all.10 = bf16[16,12,2048]{2,1,0:T(8,128)(2,1)} all-to-all(bf16[16,12,2048]{2,1,0:T(8,128)(2,1)S(1)} %reshape.273), channel_id=1, replica_groups=mesh['group'=1,'req'=4,'head'=4,'pool'=2] {'req','head'}, dimensions={0} | all-to-all | bytes 1572864 | tf_op jit(solution)/shard_map/all_to_all | solution.py:142
  88.1 1.3 reshape.274
  89.4 2.1 %fusion.26 = f32[192,384]{1,0:T(8,128)S(1)} fusion(bf16[192,2048]{1,0:T(8,128)(2,1)S(1)} %reshape.274, bf16[384,2048]{1,0:T(8,128)(2,1)} %bitcast.87), kind=kOutput, calls=%fused_computation.71 | convolution fusion | flops 301989888 | bytes 2654208 | tf_op jit(solution)/shard_map/nd,fd->nf/dot_general | solution.py:148
  91.5 0.1 fusion.6
  91.6 2.4 %convolution_convert_fusion = bf16[16,12,2048]{2,0,1:T(8,128)(2,1)} fusion(bf16[1,192,2048]{2,1,0:T(8,128)(2,1)} %param.27, bf16[16,12,192]{2,1,0:T(8,128)(2,1)S(1)} %dot_general.36), kind=kOutput, calls=%fused_computation.3 | convolution fusion | flops 151388160 | bytes 1646592 | tf_op jit(solution)/shard_map/dot_general | solution.py:152
  94.0 0.0 reduce-scatter.2.cloned.1.call-update
  94.0 6.6 %reduce-scatter.2.cloned.1.call-done = bf16[16,12,1024]{2,0,1:T(8,128)(2,1)} async-done(((bf16[16,12,2048]{2,0,1:T(8,128)(2,1)}), bf16[16,12,1024]{2,0,1:T(8,128)(2,1)}) %reduce-scatter.2.cloned.1.call-update) | async-done | bytes 393232 | tf_op jit(solution)/shard_map/reduce_scatter | solution.py:155
  100.7 2.0 %copy.63 = bf16[16,12,1024]{2,1,0:T(8,128)(2,1)} copy(bf16[16,12,1024]{2,0,1:T(8,128)(2,1)} %reduce-scatter.2.cloned.1.call-done) | data formatting | bytes 786432 | tf_op jit(solution)/shard_map/reduce_scatter | solution.py:155
  102.7 6.7 %all-to-all-start.1 = ((bf16[16,12,1024]{2,1,0:T(8,128)(2,1)}), bf16[16,12,1024]{2,1,0:T(8,128)(2,1)S(1)}, u32[]{:S(2)}, u32[]{:S(2)}) async-start(bf16[16,12,1024]{2,1,0:T(8,128)(2,1)} %copy.63), calls=%async_computation.2 | async-start | bytes 1048576 | tf_op jit(solution)/shard_map/all_to_all | solution.py:158
  109.4 15.5 %all-to-all-done.1 = bf16[16,12,1024]{2,1,0:T(8,128)(2,1)S(1)} async-done(((bf16[16,12,1024]{2,1,0:T(8,128)(2,1)}), bf16[16,12,1024]{2,1,0:T(8,128)(2,1)S(1)}, u32[]{:S(2)}, u32[]{:S(2)}) %all-to-all-start.1) | async-done | bytes 393248 | tf_op jit(solution)/shard_map/all_to_all | solution.py:158
  124.9 0.1 reshape.275
  125.0 0.9 fusion.4
  (12 shorter events, 0.1 us)
Async XLA Ops:
  6.5 15.6 %copy-start = (bf16[512,2048]{1,0:T(8,128)(2,1)S(1)}, bf16[512,2048]{1,0:T(8,128)(2,1)}, u32[]{:S(2)}) copy-start(bf16[512,2048]{1,0:T(8,128)(2,1)} %param.23) | copy-start | bytes 6291460
  6.5 8.5 %copy-start.2 = (bf16[48,2,1,256]{3,1,2,0:T(2,128)(2,1)S(1)}, bf16[48,2,1,256]{3,1,2,0:T(2,128)(2,1)}, u32[]{:S(2)}) copy-start(bf16[48,2,1,256]{3,1,2,0:T(2,128)(2,1)} %param.15) | copy-start | bytes 147460
  6.5 44.9 %all-gather.8.cloned.1.call-start = ((), (), s32[]{:S(2)}) async-start(), calls=%async_computation.4 | async-start | bytes 1769472 | tf_op jit(solution)/shard_map/all_gather | solution.py:109
  8.9 4.5 %collective-permute-start = (bf16[1,4,16,256]{3,2,1,0:T(8,128)(2,1)S(1)}, bf16[1,4,16,256]{3,2,1,0:T(8,128)(2,1)S(1)}, u32[]{:S(2)}, u32[]{:S(2)}) collective-permute-start(bf16[1,4,16,256]{3,2,1,0:T(8,128)(2,1)S(1)} %bitcast.96), channel_id=1, source_target_pairs={{0,1},{1,0},{2,3},{3,2},{4,5},{5,4},{6,7},{7,6},{8,9},{9,8},{10,11... | collective-permute-start | bytes 98312 | tf_op jit(solution)/shard_map/ppermute | solution.py:10
  21.9 1.5 %copy-start.4 = (s32[12,8]{0,1:T(8,128)S(1)}, s32[12,8]{0,1:T(8,128)}, u32[]{:S(2)}) copy-start(s32[12,8]{0,1:T(8,128)} %param.24) | copy-start | bytes 1156
  21.9 1.7 %copy-start.5 = (f32[12,8]{0,1:T(8,128)S(1)}, f32[12,8]{0,1:T(8,128)}, u32[]{:S(2)}) copy-start(f32[12,8]{0,1:T(8,128)} %param.25) | copy-start | bytes 1156
  23.3 29.8 %copy-start.1 = (bf16[12,2048]{1,0:T(8,128)(2,1)S(1)}, bf16[12,2048]{1,0:T(8,128)(2,1)}, u32[]{:S(2)}) copy-start(bf16[12,2048]{1,0:T(8,128)(2,1)} %param.21) | copy-start | bytes 147460
  23.3 30.0 %copy-start.3 = (f32[2048]{0:T(1024)S(1)}, f32[2048]{0:T(1024)}, u32[]{:S(2)}) copy-start(f32[2048]{0:T(1024)} %param.22) | copy-start | bytes 24580
  23.3 77.4 %reduce-scatter.2.cloned.1.call-start = ((), (), s32[]{:S(2)}) async-start(), calls=%async_computation.3 | async-start | bytes 1179648 | tf_op jit(solution)/shard_map/reduce_scatter | solution.py:155
  102.7 22.2 %all-to-all-start.1 = ((bf16[16,12,1024]{2,1,0:T(8,128)(2,1)}), bf16[16,12,1024]{2,1,0:T(8,128)(2,1)S(1)}, u32[]{:S(2)}, u32[]{:S(2)}) async-start(bf16[16,12,1024]{2,1,0:T(8,128)(2,1)} %copy.63), calls=%async_computation.2 | async-start | bytes 1048576 | tf_op jit(solution)/shard_map/all_to_all | solution.py:158
Sparse Core Ops, SparseCore 0:
  23.4 27.9 all-gather.7
  94.2 6.4 reduce-scatter.1
